TPU v7x, 32 devices: a whole 2x2x4 slice. The times are simulated.
32 devices in a mesh: grp: 2 (over x), orient: 16 (over z, y, core).
Axes of the slice: x: 2, y: 2, z: 4, core: 2. Of those that a mesh axis runs over, the one named last changes fastest.
Arguments:
- particles: bfloat16 [2048, 2048], P(('grp', 'orient')), parts along dimension 0, may hold values from -50 to 50
- references: bfloat16 [4096, 2048], P(('grp', 'orient')), parts along dimension 0, may hold values from -4 to 4
- tile_blocks: int32 [32, 6], P('grp'), parts along dimension 0, may hold values from 0 to 7, as said below
- tile_count: int32 [32], P('grp'), parts along dimension 0, may hold values from 1 to 6
- shift_start: int32 [32, 6], P('grp'), parts along dimension 0, may hold values from 1 to 16
Outputs:
- ref_update: float32 [4096, 2048], P(('grp', 'orient')), parts along dimension 0
- weight_sum: float32 [4096], P(('grp', 'orient')), parts along dimension 0
- log_evidence: float32 [2048], P(('grp', 'orient')), parts along dimension 0
There are 2 independent parts, one for each index of `grp`. A program takes and returns all parts, laid end to end along the dimension named above; each array names one. Nothing has to cross between parts.
Inputs may be any that keep to these rules, and one draw needn't show every extreme that they name: `tile_blocks`: in each row the first tile_count entries are distinct particle blocks, and every particle block appears among the used entries of some row.
All inputs are finite; a program needn't handle non-finite values.
Results may differ from a plain program's by a relative error of at most 0.0033.
Values may be sent and summed in bfloat16 or wider, within the bound.
A program may use at most 128 MiB of HBM per device.

v0:
```python
import math
import jax
import jax.numpy as jnp
from jax import lax
from jax.sharding import PartitionSpec as P

K = 2048
NSH = 16
TILE = 128
MOST = 6
very_negative = -1e30


def merged(array, axis, combine):
    everything = jax.tree.map(lambda part: lax.all_gather(part, axis), array)
    leading = jax.tree.map(lambda part: part[0], everything)

    def turn(k, so_far):
        return combine(so_far, jax.tree.map(lambda part: part[k], everything))

    return lax.fori_loop(1, lax.axis_size(axis), turn, leading)


def shift_phases(window_start):
    half_width = K // 2
    freq_index = jnp.arange(half_width, dtype=jnp.int32)
    freq_x = (freq_index % 32).astype(jnp.float32)
    freq_y = (freq_index // 32 - K // 128).astype(jnp.float32)
    grid_index = window_start + jnp.arange(NSH, dtype=jnp.int32)
    delta_x = (grid_index - 16).astype(jnp.float32) * 0.5
    delta_y = (5 * grid_index % 7 - 3).astype(jnp.float32) * 0.5
    angles = (
        2.0
        * math.pi
        / 64.0
        * (delta_x[:, None] * freq_x[None, :] + delta_y[:, None] * freq_y[None, :])
    )
    return (jnp.cos(angles), jnp.sin(angles))


def shifted_images(image_block, window_start):
    cosine_table, sine_table = shift_phases(window_start)
    half_width = K // 2
    real_part = image_block[:, :half_width].astype(jnp.float32)[None]
    imag_part = image_block[:, half_width:].astype(jnp.float32)[None]
    new_real = real_part * cosine_table[:, None, :] - imag_part * sine_table[:, None, :]
    new_imag = real_part * sine_table[:, None, :] + imag_part * cosine_table[:, None, :]
    stacked = jnp.concatenate([new_real, new_imag], axis=2).astype(jnp.bfloat16)
    return stacked.reshape(NSH * image_block.shape[0], K)


def tile_scores(shifted, ref_block, ref_norms):
    products = lax.dot_general(
        shifted, ref_block, (((1,), (1,)), ((), ())), preferred_element_type=jnp.float32
    )
    return (products - 0.5 * ref_norms[None, :]) / math.sqrt(K)


def combine_stats(first_pair, second_pair):
    top_first, sum_first = first_pair
    top_second, sum_second = second_pair
    top_joint = jnp.maximum(top_first, top_second)
    return (
        top_joint,
        sum_first * jnp.exp(top_first - top_joint) + sum_second * jnp.exp(top_second - top_joint),
    )


def body(particles, references, tile_blocks, tile_count, shift_start):
    local_rows = particles.shape[0]
    axis_count = lax.axis_size("orient")
    my_index = lax.axis_index("orient")
    total_rows = local_rows * axis_count
    block_total = total_rows // TILE
    ref_stack = references[None]
    lower_count = tile_count[my_index]
    ref_norms = jnp.sum(ref_stack.astype(jnp.float32) ** 2, axis=2)
    gathered = lax.all_gather(particles, "orient", axis=0, tiled=True)
    by_block = gathered.reshape(TILE, block_total, K)

    def fetch_block(block_id):
        return lax.dynamic_index_in_dim(by_block, block_id, 1, keepdims=False)

    def describe(item_index):
        in_lower = item_index < lower_count
        column = jnp.where(in_lower, my_index, my_index)
        slot_index = jnp.where(in_lower, item_index, item_index - lower_count)
        which_ref = jnp.where(column == my_index, 0, 1)
        block_id = tile_blocks[column, slot_index]
        image_block = fetch_block(block_id)
        shifted = shifted_images(image_block, shift_start[column, slot_index])
        return (which_ref, block_id, shifted)

    def first_pass(item_index, loop_state):
        score_store, running_top, running_sum = loop_state
        which_ref, block_id, shifted = describe(item_index)
        ref_block = lax.dynamic_index_in_dim(ref_stack, which_ref, 0, keepdims=False)
        norms = lax.dynamic_index_in_dim(ref_norms, which_ref, 0, keepdims=False)
        scores = tile_scores(shifted, ref_block, norms)
        by_particle = scores.reshape(NSH, TILE, TILE)
        tile_top = jnp.max(by_particle, axis=(0, 2))
        old_top = lax.dynamic_index_in_dim(running_top, block_id, 1, keepdims=False)
        old_sum = lax.dynamic_index_in_dim(running_sum, block_id, 1, keepdims=False)
        new_top = jnp.maximum(old_top, tile_top)
        tile_sum = jnp.sum(jnp.exp(by_particle - new_top[None, :, None]), axis=(0, 2))
        new_sum = old_sum * jnp.exp(old_top - new_top) + tile_sum
        running_top = lax.dynamic_update_index_in_dim(running_top, new_top, block_id, 1)
        running_sum = lax.dynamic_update_index_in_dim(running_sum, new_sum, block_id, 1)
        score_store = lax.dynamic_update_index_in_dim(score_store, scores, item_index, 0)
        return (score_store, running_top, running_sum)

    start_state = (
        jnp.zeros((MOST, NSH * TILE, TILE), jnp.float32),
        jnp.full((TILE, block_total), very_negative, jnp.float32),
        jnp.zeros((TILE, block_total), jnp.float32),
    )
    score_store, running_top, running_sum = lax.fori_loop(0, lower_count, first_pass, start_state)
    global_top, global_sum = merged((running_top, running_sum), "orient", combine_stats)

    def second_pass(item_index, loop_state):
        update_acc, weight_acc = loop_state
        which_ref, block_id, shifted = describe(item_index)
        particle_top = lax.dynamic_index_in_dim(global_top, block_id, 1, keepdims=False)
        particle_sum = lax.dynamic_index_in_dim(global_sum, block_id, 1, keepdims=False)
        item_scores = lax.dynamic_index_in_dim(score_store, item_index, 0, keepdims=False).reshape(
            NSH, TILE, TILE
        )
        weights = (
            jnp.exp(item_scores - particle_top[None, :, None]) / particle_sum[None, :, None]
        ).astype(jnp.bfloat16)
        weights = weights.reshape(NSH * TILE, TILE)
        update = lax.dot_general(
            weights, shifted, (((0,), (0,)), ((), ())), preferred_element_type=jnp.float32
        )
        weight_total = jnp.sum(weights.astype(jnp.float32), axis=0)
        current = lax.dynamic_index_in_dim(update_acc, which_ref, 0, keepdims=False)
        update_acc = lax.dynamic_update_index_in_dim(update_acc, current + update, which_ref, 0)
        current_weight = lax.dynamic_index_in_dim(weight_acc, which_ref, 0, keepdims=False)
        weight_acc = lax.dynamic_update_index_in_dim(
            weight_acc, current_weight + weight_total, which_ref, 0
        )
        return (update_acc, weight_acc)

    stack_depth = ref_stack.shape[0]
    back_state = (
        jnp.zeros((stack_depth, TILE, K), jnp.float32),
        jnp.zeros((stack_depth, TILE), jnp.float32),
    )
    update_acc, weight_acc = lax.fori_loop(0, lower_count, second_pass, back_state)
    ref_update = update_acc[0]
    weight_sum = weight_acc[0]
    evidence = (global_top + jnp.log(global_sum)).reshape(total_rows)
    log_evidence = lax.dynamic_slice_in_dim(evidence, my_index * local_rows, local_rows, 0)
    return (ref_update, weight_sum, log_evidence)


def solution(mesh):
    in_specs = (
        P(("grp", "orient"), None),
        P(("grp", "orient"), None),
        P("grp", None),
        P("grp"),
        P("grp", None),
    )
    out_specs = (P(("grp", "orient"), None), P(("grp", "orient")), P(("grp", "orient")))
    return jax.shard_map(body, mesh=mesh, in_specs=in_specs, out_specs=out_specs, check_vma=False)
```

profile of v0, /device:TPU:30, one launch (start us, length us, event | category | flops | bytes accessed | tf_op | source)
XLA Modules:
  0.0 364.0 jit_solution(5189252617112790068)
XLA Ops:
  10.4 48.7 %all-gather.4.cloned.1.call-done = bf16[1024,2048]{1,0:T(8,128)(2,1)} async-done(((bf16[64,2048]{1,0:T(8,128)(2,1)}), bf16[1024,2048]{1,0:T(8,128)(2,1)}) %all-gather.4.cloned.1.call-update) | async-done | bytes 4194320 | tf_op jit(solution)/shard_map/all_gather | solution.py:78
  59.1 6.6 %copy.16 = bf16[128,8,2048]{2,0,1:T(8,128)(2,1)} copy(bf16[128,8,2048]{2,1,0:T(8,128)(2,1)} %bitcast.141) | data formatting | bytes 8388608 | tf_op jit(solution)/shard_map/while | solution.py:117
  65.6 3.4 broadcast_in_dim.45
  69.1 127.2 %while.49 = (s32[]{:T(128)}, f32[6,2048,128]{1,2,0:T(8,128)}, f32[128,8]{0,1:T(8,128)S(1)}, f32[128,8]{0,1:T(8,128)S(1)}, s32[]{:T(128)}, /*index=5*/s32[16,6]{0...) while((s32[]{:T(128)}, f32[6,2048,128]{1,2,0:T(8,128)}, ...), condition=%wide.region_6.7_spmd, body=%wide.region_1.6_spmd.sunk | while | flops 1108950784 | bytes 25503828 | solution.py:117
  77.6 4.8 %subtract_convert_fusion.4 = (bf16[16,128,1024]{2,1,0:T(8,128)(2,1)}, bf16[16,128,1024]{2,1,0:T(8,128)(2,1)}) fusion(f32[16,1024]{1,0:T(8,128)S(1)} %get-tuple-element.877, f32[128,1024]{1,0:T(8,128)S(1)} %get-tuple-element.878, f32[16,1024]{1,0:T(8,128)S(1)} %get-tuple-element.879, f32[128,1024]{1,0:T(8,128)S(1)} %get-tuple-element.880), kind=kLoop, calls=%fused_computation.5.clone.1 | loop fusion | flops 16777216 | bytes 9568256 | tf_op jit(solution)/shard_map/convert.3
  82.4 7.3 %bitcast_dynamic-update-slice_fusion.2 = (f32[6,2048,128]{1,2,0:T(8,128)}, f32[2048,128]{0,1:T(8,128)S(1)}) fusion(f32[6,2048,128]{1,2,0:T(8,128)} %get-tuple-element.934, s32[]{:T(128)S(6)} %select_n.243, f32[128]{0:T(128)S(1)} %multiply_bitcast_fusion.2, bf16[1,128,2048]{2,1,0:T(8,128)(2,1)S(1)} %get-tuple-element.958, ...), kind=kOutput, calls=%fused_computation.8.clone.1 | convolution fusion | flops 1091043328 | bytes 11010564 | tf_op jit(solution)/shard_map/while/body/dot_general | solution.py:53
  98.7 4.8 %subtract_convert_fusion.4 = (bf16[16,128,1024]{2,1,0:T(8,128)(2,1)}, bf16[16,128,1024]{2,1,0:T(8,128)(2,1)}) fusion(f32[16,1024]{1,0:T(8,128)S(1)} %get-tuple-element.877, f32[128,1024]{1,0:T(8,128)S(1)} %get-tuple-element.878, f32[16,1024]{1,0:T(8,128)S(1)} %get-tuple-element.879, f32[128,1024]{1,0:T(8,128)S(1)} %get-tuple-element.880), kind=kLoop, calls=%fused_computation.5.clone.1 | loop fusion | flops 16777216 | bytes 9568256 | tf_op jit(solution)/shard_map/convert.3
  103.5 7.4 %bitcast_dynamic-update-slice_fusion.2 = (f32[6,2048,128]{1,2,0:T(8,128)}, f32[2048,128]{0,1:T(8,128)S(1)}) fusion(f32[6,2048,128]{1,2,0:T(8,128)} %get-tuple-element.934, s32[]{:T(128)S(6)} %select_n.243, f32[128]{0:T(128)S(1)} %multiply_bitcast_fusion.2, bf16[1,128,2048]{2,1,0:T(8,128)(2,1)S(1)} %get-tuple-element.958, ...), kind=kOutput, calls=%fused_computation.8.clone.1 | convolution fusion | flops 1091043328 | bytes 11010564 | tf_op jit(solution)/shard_map/while/body/dot_general | solution.py:53
  119.8 4.8 %subtract_convert_fusion.4 = (bf16[16,128,1024]{2,1,0:T(8,128)(2,1)}, bf16[16,128,1024]{2,1,0:T(8,128)(2,1)}) fusion(f32[16,1024]{1,0:T(8,128)S(1)} %get-tuple-element.877, f32[128,1024]{1,0:T(8,128)S(1)} %get-tuple-element.878, f32[16,1024]{1,0:T(8,128)S(1)} %get-tuple-element.879, f32[128,1024]{1,0:T(8,128)S(1)} %get-tuple-element.880), kind=kLoop, calls=%fused_computation.5.clone.1 | loop fusion | flops 16777216 | bytes 9568256 | tf_op jit(solution)/shard_map/convert.3
  124.6 7.4 %bitcast_dynamic-update-slice_fusion.2 = (f32[6,2048,128]{1,2,0:T(8,128)}, f32[2048,128]{0,1:T(8,128)S(1)}) fusion(f32[6,2048,128]{1,2,0:T(8,128)} %get-tuple-element.934, s32[]{:T(128)S(6)} %select_n.243, f32[128]{0:T(128)S(1)} %multiply_bitcast_fusion.2, bf16[1,128,2048]{2,1,0:T(8,128)(2,1)S(1)} %get-tuple-element.958, ...), kind=kOutput, calls=%fused_computation.8.clone.1 | convolution fusion | flops 1091043328 | bytes 11010564 | tf_op jit(solution)/shard_map/while/body/dot_general | solution.py:53
  140.9 4.8 %subtract_convert_fusion.4 = (bf16[16,128,1024]{2,1,0:T(8,128)(2,1)}, bf16[16,128,1024]{2,1,0:T(8,128)(2,1)}) fusion(f32[16,1024]{1,0:T(8,128)S(1)} %get-tuple-element.877, f32[128,1024]{1,0:T(8,128)S(1)} %get-tuple-element.878, f32[16,1024]{1,0:T(8,128)S(1)} %get-tuple-element.879, f32[128,1024]{1,0:T(8,128)S(1)} %get-tuple-element.880), kind=kLoop, calls=%fused_computation.5.clone.1 | loop fusion | flops 16777216 | bytes 9568256 | tf_op jit(solution)/shard_map/convert.3
  145.7 7.3 %bitcast_dynamic-update-slice_fusion.2 = (f32[6,2048,128]{1,2,0:T(8,128)}, f32[2048,128]{0,1:T(8,128)S(1)}) fusion(f32[6,2048,128]{1,2,0:T(8,128)} %get-tuple-element.934, s32[]{:T(128)S(6)} %select_n.243, f32[128]{0:T(128)S(1)} %multiply_bitcast_fusion.2, bf16[1,128,2048]{2,1,0:T(8,128)(2,1)S(1)} %get-tuple-element.958, ...), kind=kOutput, calls=%fused_computation.8.clone.1 | convolution fusion | flops 1091043328 | bytes 11010564 | tf_op jit(solution)/shard_map/while/body/dot_general | solution.py:53
  162.0 4.8 %subtract_convert_fusion.4 = (bf16[16,128,1024]{2,1,0:T(8,128)(2,1)}, bf16[16,128,1024]{2,1,0:T(8,128)(2,1)}) fusion(f32[16,1024]{1,0:T(8,128)S(1)} %get-tuple-element.877, f32[128,1024]{1,0:T(8,128)S(1)} %get-tuple-element.878, f32[16,1024]{1,0:T(8,128)S(1)} %get-tuple-element.879, f32[128,1024]{1,0:T(8,128)S(1)} %get-tuple-element.880), kind=kLoop, calls=%fused_computation.5.clone.1 | loop fusion | flops 16777216 | bytes 9568256 | tf_op jit(solution)/shard_map/convert.3
  166.8 7.4 %bitcast_dynamic-update-slice_fusion.2 = (f32[6,2048,128]{1,2,0:T(8,128)}, f32[2048,128]{0,1:T(8,128)S(1)}) fusion(f32[6,2048,128]{1,2,0:T(8,128)} %get-tuple-element.934, s32[]{:T(128)S(6)} %select_n.243, f32[128]{0:T(128)S(1)} %multiply_bitcast_fusion.2, bf16[1,128,2048]{2,1,0:T(8,128)(2,1)S(1)} %get-tuple-element.958, ...), kind=kOutput, calls=%fused_computation.8.clone.1 | convolution fusion | flops 1091043328 | bytes 11010564 | tf_op jit(solution)/shard_map/while/body/dot_general | solution.py:53
  183.0 4.8 %subtract_convert_fusion.4 = (bf16[16,128,1024]{2,1,0:T(8,128)(2,1)}, bf16[16,128,1024]{2,1,0:T(8,128)(2,1)}) fusion(f32[16,1024]{1,0:T(8,128)S(1)} %get-tuple-element.877, f32[128,1024]{1,0:T(8,128)S(1)} %get-tuple-element.878, f32[16,1024]{1,0:T(8,128)S(1)} %get-tuple-element.879, f32[128,1024]{1,0:T(8,128)S(1)} %get-tuple-element.880), kind=kLoop, calls=%fused_computation.5.clone.1 | loop fusion | flops 16777216 | bytes 9568256 | tf_op jit(solution)/shard_map/convert.3
  187.8 7.4 %bitcast_dynamic-update-slice_fusion.2 = (f32[6,2048,128]{1,2,0:T(8,128)}, f32[2048,128]{0,1:T(8,128)S(1)}) fusion(f32[6,2048,128]{1,2,0:T(8,128)} %get-tuple-element.934, s32[]{:T(128)S(6)} %select_n.243, f32[128]{0:T(128)S(1)} %multiply_bitcast_fusion.2, bf16[1,128,2048]{2,1,0:T(8,128)(2,1)S(1)} %get-tuple-element.958, ...), kind=kOutput, calls=%fused_computation.8.clone.1 | convolution fusion | flops 1091043328 | bytes 11010564 | tf_op jit(solution)/shard_map/while/body/dot_general | solution.py:53
  196.3 16.7 %all-gather = f32[2048,8]{0,1:T(8,128)S(1)} all-gather(f32[128,8]{0,1:T(8,128)S(1)} %get-tuple-element.540), channel_id=2, replica_groups=mesh['grp'=2,'orient'=16] {'orient'}, dimensions={0}, use_global_device_ids=true | all-gather | bytes 69632 | tf_op jit(solution)/shard_map/all_gather | solution.py:15
  212.9 19.8 %all-gather.1 = f32[2048,8]{0,1:T(8,128)S(1)} all-gather(f32[128,8]{0,1:T(8,128)S(1)} %get-tuple-element.541), channel_id=3, replica_groups=mesh['grp'=2,'orient'=16] {'orient'}, dimensions={0}, use_global_device_ids=true | all-gather | bytes 69632 | tf_op jit(solution)/shard_map/all_gather | solution.py:15
  233.7 122.5 %while.51 = (s32[]{:T(128)}, f32[1,128,2048]{2,1,0:T(8,128)S(1)}, f32[1,128]{1,0:T(1,128)S(1)}, s32[]{:T(128)}, f32[6,2048,128]{1,2,0:T(8,128)}, /*index=5*/s32[...) while((s32[]{:T(128)}, f32[1,128,2048]{2,1,0:T(8,128)S(1)}, ...), condition=%wide.region_11.12_spmd, body=%wide.region_9.11_spmd.sunk | while | flops 1109998848 | bytes 29153852 | solution.py:149
  242.2 4.8 %subtract_convert_fusion.5 = (bf16[16,128,1024]{2,1,0:T(8,128)(2,1)}, bf16[16,128,1024]{2,1,0:T(8,128)(2,1)}) fusion(f32[16,1024]{1,0:T(8,128)S(1)} %get-tuple-element.909, f32[128,1024]{1,0:T(8,128)S(1)} %get-tuple-element.910, f32[16,1024]{1,0:T(8,128)S(1)} %get-tuple-element.911, f32[128,1024]{1,0:T(8,128)S(1)} %get-tuple-element.912), kind=kLoop, calls=%fused_computation.57.clone.1 | loop fusion | flops 16777216 | bytes 9568256 | tf_op jit(solution)/shard_map/convert.4
  247.0 1.3 constant_dynamic-slice_fusion.6
  248.7 4.6 %fusion.84 = f32[1,128,2048]{2,1,0:T(8,128)S(1)} fusion(bf16[16,128,1024]{2,1,0:T(8,128)(2,1)} %get-tuple-element.913, bf16[16,128,1024]{2,1,0:T(8,128)(2,1)} %get-tuple-element.914, f32[1,128,2048]{2,1,0:T(8,128)S(1)} %get-tuple-element.1005, f32[16,128,128]{2,1,0:T(8,128)S(1)} %bitcast.140, f32[128]{0:T(128)S(1)} %get-tuple-element.915, ...), kind=kOutput, calls=%fused_computation.60.clone.1 | convolution fusion | flops 1091567616 | bytes 11535360 | tf_op jit(solution)/shard_map/while/body/dot_general | solution.py:132
  262.6 4.8 %subtract_convert_fusion.5 = (bf16[16,128,1024]{2,1,0:T(8,128)(2,1)}, bf16[16,128,1024]{2,1,0:T(8,128)(2,1)}) fusion(f32[16,1024]{1,0:T(8,128)S(1)} %get-tuple-element.909, f32[128,1024]{1,0:T(8,128)S(1)} %get-tuple-element.910, f32[16,1024]{1,0:T(8,128)S(1)} %get-tuple-element.911, f32[128,1024]{1,0:T(8,128)S(1)} %get-tuple-element.912), kind=kLoop, calls=%fused_computation.57.clone.1 | loop fusion | flops 16777216 | bytes 9568256 | tf_op jit(solution)/shard_map/convert.4
  269.0 4.6 %fusion.84 = f32[1,128,2048]{2,1,0:T(8,128)S(1)} fusion(bf16[16,128,1024]{2,1,0:T(8,128)(2,1)} %get-tuple-element.913, bf16[16,128,1024]{2,1,0:T(8,128)(2,1)} %get-tuple-element.914, f32[1,128,2048]{2,1,0:T(8,128)S(1)} %get-tuple-element.1005, f32[16,128,128]{2,1,0:T(8,128)S(1)} %bitcast.140, f32[128]{0:T(128)S(1)} %get-tuple-element.915, ...), kind=kOutput, calls=%fused_computation.60.clone.1 | convolution fusion | flops 1091567616 | bytes 11535360 | tf_op jit(solution)/shard_map/while/body/dot_general | solution.py:132
  282.9 4.8 %subtract_convert_fusion.5 = (bf16[16,128,1024]{2,1,0:T(8,128)(2,1)}, bf16[16,128,1024]{2,1,0:T(8,128)(2,1)}) fusion(f32[16,1024]{1,0:T(8,128)S(1)} %get-tuple-element.909, f32[128,1024]{1,0:T(8,128)S(1)} %get-tuple-element.910, f32[16,1024]{1,0:T(8,128)S(1)} %get-tuple-element.911, f32[128,1024]{1,0:T(8,128)S(1)} %get-tuple-element.912), kind=kLoop, calls=%fused_computation.57.clone.1 | loop fusion | flops 16777216 | bytes 9568256 | tf_op jit(solution)/shard_map/convert.4
  289.3 4.6 %fusion.84 = f32[1,128,2048]{2,1,0:T(8,128)S(1)} fusion(bf16[16,128,1024]{2,1,0:T(8,128)(2,1)} %get-tuple-element.913, bf16[16,128,1024]{2,1,0:T(8,128)(2,1)} %get-tuple-element.914, f32[1,128,2048]{2,1,0:T(8,128)S(1)} %get-tuple-element.1005, f32[16,128,128]{2,1,0:T(8,128)S(1)} %bitcast.140, f32[128]{0:T(128)S(1)} %get-tuple-element.915, ...), kind=kOutput, calls=%fused_computation.60.clone.1 | convolution fusion | flops 1091567616 | bytes 11535360 | tf_op jit(solution)/shard_map/while/body/dot_general | solution.py:132
  303.2 4.8 %subtract_convert_fusion.5 = (bf16[16,128,1024]{2,1,0:T(8,128)(2,1)}, bf16[16,128,1024]{2,1,0:T(8,128)(2,1)}) fusion(f32[16,1024]{1,0:T(8,128)S(1)} %get-tuple-element.909, f32[128,1024]{1,0:T(8,128)S(1)} %get-tuple-element.910, f32[16,1024]{1,0:T(8,128)S(1)} %get-tuple-element.911, f32[128,1024]{1,0:T(8,128)S(1)} %get-tuple-element.912), kind=kLoop, calls=%fused_computation.57.clone.1 | loop fusion | flops 16777216 | bytes 9568256 | tf_op jit(solution)/shard_map/convert.4
  309.6 4.6 %fusion.84 = f32[1,128,2048]{2,1,0:T(8,128)S(1)} fusion(bf16[16,128,1024]{2,1,0:T(8,128)(2,1)} %get-tuple-element.913, bf16[16,128,1024]{2,1,0:T(8,128)(2,1)} %get-tuple-element.914, f32[1,128,2048]{2,1,0:T(8,128)S(1)} %get-tuple-element.1005, f32[16,128,128]{2,1,0:T(8,128)S(1)} %bitcast.140, f32[128]{0:T(128)S(1)} %get-tuple-element.915, ...), kind=kOutput, calls=%fused_computation.60.clone.1 | convolution fusion | flops 1091567616 | bytes 11535360 | tf_op jit(solution)/shard_map/while/body/dot_general | solution.py:132
  323.5 4.8 %subtract_convert_fusion.5 = (bf16[16,128,1024]{2,1,0:T(8,128)(2,1)}, bf16[16,128,1024]{2,1,0:T(8,128)(2,1)}) fusion(f32[16,1024]{1,0:T(8,128)S(1)} %get-tuple-element.909, f32[128,1024]{1,0:T(8,128)S(1)} %get-tuple-element.910, f32[16,1024]{1,0:T(8,128)S(1)} %get-tuple-element.911, f32[128,1024]{1,0:T(8,128)S(1)} %get-tuple-element.912), kind=kLoop, calls=%fused_computation.57.clone.1 | loop fusion | flops 16777216 | bytes 9568256 | tf_op jit(solution)/shard_map/convert.4
  329.9 4.6 %fusion.84 = f32[1,128,2048]{2,1,0:T(8,128)S(1)} fusion(bf16[16,128,1024]{2,1,0:T(8,128)(2,1)} %get-tuple-element.913, bf16[16,128,1024]{2,1,0:T(8,128)(2,1)} %get-tuple-element.914, f32[1,128,2048]{2,1,0:T(8,128)S(1)} %get-tuple-element.1005, f32[16,128,128]{2,1,0:T(8,128)S(1)} %bitcast.140, f32[128]{0:T(128)S(1)} %get-tuple-element.915, ...), kind=kOutput, calls=%fused_computation.60.clone.1 | convolution fusion | flops 1091567616 | bytes 11535360 | tf_op jit(solution)/shard_map/while/body/dot_general | solution.py:132
  343.8 4.8 %subtract_convert_fusion.5 = (bf16[16,128,1024]{2,1,0:T(8,128)(2,1)}, bf16[16,128,1024]{2,1,0:T(8,128)(2,1)}) fusion(f32[16,1024]{1,0:T(8,128)S(1)} %get-tuple-element.909, f32[128,1024]{1,0:T(8,128)S(1)} %get-tuple-element.910, f32[16,1024]{1,0:T(8,128)S(1)} %get-tuple-element.911, f32[128,1024]{1,0:T(8,128)S(1)} %get-tuple-element.912), kind=kLoop, calls=%fused_computation.57.clone.1 | loop fusion | flops 16777216 | bytes 9568256 | tf_op jit(solution)/shard_map/convert.4
  350.2 4.6 %fusion.84 = f32[1,128,2048]{2,1,0:T(8,128)S(1)} fusion(bf16[16,128,1024]{2,1,0:T(8,128)(2,1)} %get-tuple-element.913, bf16[16,128,1024]{2,1,0:T(8,128)(2,1)} %get-tuple-element.914, f32[1,128,2048]{2,1,0:T(8,128)S(1)} %get-tuple-element.1005, f32[16,128,128]{2,1,0:T(8,128)S(1)} %bitcast.140, f32[128]{0:T(128)S(1)} %get-tuple-element.915, ...), kind=kOutput, calls=%fused_computation.60.clone.1 | convolution fusion | flops 1091567616 | bytes 11535360 | tf_op jit(solution)/shard_map/while/body/dot_general | solution.py:132
  (221 shorter events, 76.9 us)
Async XLA Ops:
  7.2 51.9 %all-gather.4.cloned.1.call-start = ((), (), s32[]{:S(2)}) async-start(), calls=%async_computation | async-start | bytes 4456448 | tf_op jit(solution)/shard_map/all_gather | solution.py:78
  59.1 10.0 %copy-start.1 = (bf16[128,2048]{1,0:T(8,128)(2,1)S(1)}, bf16[128,2048]{1,0:T(8,128)(2,1)}, u32[]{:S(2)}) copy-start(bf16[128,2048]{1,0:T(8,128)(2,1)} %param.12) | copy-start | bytes 1572868
  356.2 1.0 copy-start
  356.2 1.0 copy-start.2
Sparse Core Ops, SparseCore 0:
  10.1 48.8 all-gather.3
where the time goes:
time: 366 us; the launch traced here: 364 us
  other arithmetic  77.9 us (21%)
  matrix products  71.5 us (20%)
  local copies, waits for them, and re-layouts  66.5 us (18%)
  waiting for transfers between devices  49.4 us (13%)
  loops' own time  48.1 us (13%)
  blocking collectives  36.5 us (10%)
  between operations  14.1 us (4%)
    another operation x12, other arithmetic  57.5 us
    all_gather x1, waiting for transfers between devices, body(): gathered = lax.all_gather(particles, 'orient', axis=0, tiled=True)  48.7 us
    dot_general x6, matrix products, tile_scores(): lax.dot_general(shifted, ref_block, (((1,), (1,)), ((), ())), preferred_e...  44.2 us
    all_gather x2, blocking collectives, merged(): everything = jax.tree.map(lambda part: lax.all_gather(part, axis), array)  36.5 us
    dot_general x6, matrix products, second_pass(): lax.dot_general(weights, shifted, (((0,), (0,)), ((), ())), preferred_ele...  27.3 us
    another operation x1, loops' own time, body(): lax.fori_loop(0, lower_count, second_pass, back_state)  24 us
    another operation x1, loops' own time, body(): lax.fori_loop(0, lower_count, first_pass, start_state)  23.8 us
    dynamic_slice x12, local copies, waits for them, and re-layouts, describe(): block_id = tile_blocks[column, slot_index]  15.4 us
  transfers between devices with their start and end apart: 1, of which 1 were waited for; matrix products, arithmetic and copies ran while one was open for 1% of the time, Pallas kernels for 0%

commit v1 on v0

--- a/solution.py
+++ b/solution.py
@@ -75,7 +75,15 @@
     ref_stack = references[None]
     lower_count = tile_count[my_index]
     ref_norms = jnp.sum(ref_stack.astype(jnp.float32) ** 2, axis=2)
-    gathered = lax.all_gather(particles, "orient", axis=0, tiled=True)
+    ways, here, step = (lax.axis_size("orient"), lax.axis_index("orient"), particles.shape[0])
+    line, have = (particles, 1)
+    while have < ways:
+        line = jnp.concatenate(
+            [line, lax.ppermute(line, "orient", [(d, (d - have) % ways) for d in range(ways)])],
+            axis=0,
+        )
+        have = 2 * have
+    gathered = jnp.roll(line, here * step, axis=0)
     by_block = gathered.reshape(TILE, block_total, K)
 
     def fetch_block(block_id):

time: 366 us -> 441 us (1.20)
  waiting for transfers between devices: 49.4 us -> 129 us
  between operations: 14.1 us -> 0.84 us
  other arithmetic: 77.9 us -> 83.2 us
    ppermute x0 -> x4, waiting for transfers between devices: none -> 129 us  [body(): lax.ppermute(line, 'orient', [(d, (d - have) % ways) for d in range(ways)])]
    all_gather x1 -> x0, waiting for transfers between devices: 48.7 us -> none  [body(): gathered = lax.all_gather(particles, 'orient', axis=0, tiled=True)]
    concatenate x0 -> x3, other arithmetic: none -> 4.71 us  [body(): jnp.concatenate([line, lax.ppermute(line, 'orient', [(d, (d - have) % way...]
  transfers between devices with their start and end apart: 1 -> 4, of which waited for: 1 -> 4; matrix products, arithmetic and copies ran while one was open for 1% -> 1% of each run, Pallas kernels for 0% -> 0%
where the time goes in v1:
time: 441 us; the launch traced here: 438 us
  waiting for transfers between devices  129 us (29%)
  other arithmetic  83.2 us (19%)
  matrix products  71.5 us (16%)
  local copies, waits for them, and re-layouts  68.3 us (15%)
  loops' own time  46.6 us (11%)
  blocking collectives  36.5 us (8%)
    ppermute x4, waiting for transfers between devices, body(): lax.ppermute(line, 'orient', [(d, (d - have) % ways) for d in range(ways)])  129 us
    another operation x12, other arithmetic  57.8 us
    dot_general x6, matrix products, tile_scores(): lax.dot_general(shifted, ref_block, (((1,), (1,)), ((), ())), preferred_e...  44.2 us
    all_gather x2, blocking collectives, merged(): everything = jax.tree.map(lambda part: lax.all_gather(part, axis), array)  36.5 us
    dot_general x6, matrix products, second_pass(): lax.dot_general(weights, shifted, (((0,), (0,)), ((), ())), preferred_ele...  27.3 us
    another operation x1, loops' own time, body(): lax.fori_loop(0, lower_count, second_pass, back_state)  23.3 us
    another operation x1, loops' own time, body(): lax.fori_loop(0, lower_count, first_pass, start_state)  23 us
    dynamic_slice x12, local copies, waits for them, and re-layouts, describe(): block_id = tile_blocks[column, slot_index]  15.3 us
  transfers between devices with their start and end apart: 4, of which 4 were waited for; matrix products, arithmetic and copies ran while one was open for 1% of the time, Pallas kernels for 0%

profile of v1, /device:TPU:30, one launch (start us, length us, event | category | flops | bytes accessed | tf_op | source)
XLA Modules:
  0.0 438.1 jit_solution(13681935178760060273)
XLA Ops:
  7.4 12.8 %collective-permute-done.1 = bf16[128,2048]{1,0:T(8,128)(2,1)S(1)} collective-permute-done((bf16[128,2048]{1,0:T(8,128)(2,1)S(1)}, bf16[128,2048]{1,0:T(8,128)(2,1)S(1)}, u32[]{:S(2)}, u32[]{:S(2)}) %collective-permute-start.1) | collective-permute-done | bytes 524320 | tf_op jit(solution)/shard_map/ppermute | solution.py:82
  21.9 25.2 %collective-permute-done.2 = bf16[256,2048]{1,0:T(8,128)(2,1)S(1)} collective-permute-done((bf16[256,2048]{1,0:T(8,128)(2,1)S(1)}, bf16[256,2048]{1,0:T(8,128)(2,1)S(1)}, u32[]{:S(2)}, u32[]{:S(2)}) %collective-permute-start.2) | collective-permute-done | bytes 1048608 | tf_op jit(solution)/shard_map/ppermute | solution.py:82
  55.5 86.7 %collective-permute-done.3 = bf16[512,2048]{1,0:T(8,128)(2,1)S(1)} collective-permute-done((bf16[512,2048]{1,0:T(8,128)(2,1)}, bf16[512,2048]{1,0:T(8,128)(2,1)S(1)}, u32[]{:S(2)}, u32[]{:S(2)}) %collective-permute-start.3) | collective-permute-done | bytes 2097184 | tf_op jit(solution)/shard_map/ppermute | solution.py:82
  143.3 4.3 copy.16
  151.1 126.6 %while.49 = (s32[]{:T(128)}, f32[6,2048,128]{1,2,0:T(8,128)}, f32[128,8]{0,1:T(8,128)S(1)}, f32[128,8]{0,1:T(8,128)S(1)}, s32[]{:T(128)}, /*index=5*/s32[16,6]{0...) while((s32[]{:T(128)}, f32[6,2048,128]{1,2,0:T(8,128)}, ...), condition=%wide.region_6.7_spmd, body=%wide.region_1.6_spmd.sunk | while | flops 1108950784 | bytes 25503828 | solution.py:125
  159.6 4.8 %subtract_convert_fusion.4 = (bf16[16,128,1024]{2,1,0:T(8,128)(2,1)}, bf16[16,128,1024]{2,1,0:T(8,128)(2,1)}) fusion(f32[16,1024]{1,0:T(8,128)S(1)} %get-tuple-element.877, f32[128,1024]{1,0:T(8,128)S(1)} %get-tuple-element.878, f32[16,1024]{1,0:T(8,128)S(1)} %get-tuple-element.879, f32[128,1024]{1,0:T(8,128)S(1)} %get-tuple-element.880), kind=kLoop, calls=%fused_computation.5.clone.1 | loop fusion | flops 16777216 | bytes 9568256 | tf_op jit(solution)/shard_map/convert.3
  164.4 7.3 %bitcast_dynamic-update-slice_fusion.2 = (f32[6,2048,128]{1,2,0:T(8,128)}, f32[2048,128]{0,1:T(8,128)S(1)}) fusion(f32[6,2048,128]{1,2,0:T(8,128)} %get-tuple-element.934, s32[]{:T(128)S(6)} %select_n.258, f32[128]{0:T(128)S(1)} %multiply_bitcast_fusion.2, bf16[1,128,2048]{2,1,0:T(8,128)(2,1)S(1)} %get-tuple-element.958, ...), kind=kOutput, calls=%fused_computation.8.clone.1 | convolution fusion | flops 1091043328 | bytes 11010564 | tf_op jit(solution)/shard_map/while/body/dot_general | solution.py:53
  180.5 4.8 %subtract_convert_fusion.4 = (bf16[16,128,1024]{2,1,0:T(8,128)(2,1)}, bf16[16,128,1024]{2,1,0:T(8,128)(2,1)}) fusion(f32[16,1024]{1,0:T(8,128)S(1)} %get-tuple-element.877, f32[128,1024]{1,0:T(8,128)S(1)} %get-tuple-element.878, f32[16,1024]{1,0:T(8,128)S(1)} %get-tuple-element.879, f32[128,1024]{1,0:T(8,128)S(1)} %get-tuple-element.880), kind=kLoop, calls=%fused_computation.5.clone.1 | loop fusion | flops 16777216 | bytes 9568256 | tf_op jit(solution)/shard_map/convert.3
  185.3 7.4 %bitcast_dynamic-update-slice_fusion.2 = (f32[6,2048,128]{1,2,0:T(8,128)}, f32[2048,128]{0,1:T(8,128)S(1)}) fusion(f32[6,2048,128]{1,2,0:T(8,128)} %get-tuple-element.934, s32[]{:T(128)S(6)} %select_n.258, f32[128]{0:T(128)S(1)} %multiply_bitcast_fusion.2, bf16[1,128,2048]{2,1,0:T(8,128)(2,1)S(1)} %get-tuple-element.958, ...), kind=kOutput, calls=%fused_computation.8.clone.1 | convolution fusion | flops 1091043328 | bytes 11010564 | tf_op jit(solution)/shard_map/while/body/dot_general | solution.py:53
  201.5 4.8 %subtract_convert_fusion.4 = (bf16[16,128,1024]{2,1,0:T(8,128)(2,1)}, bf16[16,128,1024]{2,1,0:T(8,128)(2,1)}) fusion(f32[16,1024]{1,0:T(8,128)S(1)} %get-tuple-element.877, f32[128,1024]{1,0:T(8,128)S(1)} %get-tuple-element.878, f32[16,1024]{1,0:T(8,128)S(1)} %get-tuple-element.879, f32[128,1024]{1,0:T(8,128)S(1)} %get-tuple-element.880), kind=kLoop, calls=%fused_computation.5.clone.1 | loop fusion | flops 16777216 | bytes 9568256 | tf_op jit(solution)/shard_map/convert.3
  206.4 7.4 %bitcast_dynamic-update-slice_fusion.2 = (f32[6,2048,128]{1,2,0:T(8,128)}, f32[2048,128]{0,1:T(8,128)S(1)}) fusion(f32[6,2048,128]{1,2,0:T(8,128)} %get-tuple-element.934, s32[]{:T(128)S(6)} %select_n.258, f32[128]{0:T(128)S(1)} %multiply_bitcast_fusion.2, bf16[1,128,2048]{2,1,0:T(8,128)(2,1)S(1)} %get-tuple-element.958, ...), kind=kOutput, calls=%fused_computation.8.clone.1 | convolution fusion | flops 1091043328 | bytes 11010564 | tf_op jit(solution)/shard_map/while/body/dot_general | solution.py:53
  222.5 4.8 %subtract_convert_fusion.4 = (bf16[16,128,1024]{2,1,0:T(8,128)(2,1)}, bf16[16,128,1024]{2,1,0:T(8,128)(2,1)}) fusion(f32[16,1024]{1,0:T(8,128)S(1)} %get-tuple-element.877, f32[128,1024]{1,0:T(8,128)S(1)} %get-tuple-element.878, f32[16,1024]{1,0:T(8,128)S(1)} %get-tuple-element.879, f32[128,1024]{1,0:T(8,128)S(1)} %get-tuple-element.880), kind=kLoop, calls=%fused_computation.5.clone.1 | loop fusion | flops 16777216 | bytes 9568256 | tf_op jit(solution)/shard_map/convert.3
  227.4 7.4 %bitcast_dynamic-update-slice_fusion.2 = (f32[6,2048,128]{1,2,0:T(8,128)}, f32[2048,128]{0,1:T(8,128)S(1)}) fusion(f32[6,2048,128]{1,2,0:T(8,128)} %get-tuple-element.934, s32[]{:T(128)S(6)} %select_n.258, f32[128]{0:T(128)S(1)} %multiply_bitcast_fusion.2, bf16[1,128,2048]{2,1,0:T(8,128)(2,1)S(1)} %get-tuple-element.958, ...), kind=kOutput, calls=%fused_computation.8.clone.1 | convolution fusion | flops 1091043328 | bytes 11010564 | tf_op jit(solution)/shard_map/while/body/dot_general | solution.py:53
  243.6 4.8 %subtract_convert_fusion.4 = (bf16[16,128,1024]{2,1,0:T(8,128)(2,1)}, bf16[16,128,1024]{2,1,0:T(8,128)(2,1)}) fusion(f32[16,1024]{1,0:T(8,128)S(1)} %get-tuple-element.877, f32[128,1024]{1,0:T(8,128)S(1)} %get-tuple-element.878, f32[16,1024]{1,0:T(8,128)S(1)} %get-tuple-element.879, f32[128,1024]{1,0:T(8,128)S(1)} %get-tuple-element.880), kind=kLoop, calls=%fused_computation.5.clone.1 | loop fusion | flops 16777216 | bytes 9568256 | tf_op jit(solution)/shard_map/convert.3
  248.4 7.3 %bitcast_dynamic-update-slice_fusion.2 = (f32[6,2048,128]{1,2,0:T(8,128)}, f32[2048,128]{0,1:T(8,128)S(1)}) fusion(f32[6,2048,128]{1,2,0:T(8,128)} %get-tuple-element.934, s32[]{:T(128)S(6)} %select_n.258, f32[128]{0:T(128)S(1)} %multiply_bitcast_fusion.2, bf16[1,128,2048]{2,1,0:T(8,128)(2,1)S(1)} %get-tuple-element.958, ...), kind=kOutput, calls=%fused_computation.8.clone.1 | convolution fusion | flops 1091043328 | bytes 11010564 | tf_op jit(solution)/shard_map/while/body/dot_general | solution.py:53
  264.5 4.8 %subtract_convert_fusion.4 = (bf16[16,128,1024]{2,1,0:T(8,128)(2,1)}, bf16[16,128,1024]{2,1,0:T(8,128)(2,1)}) fusion(f32[16,1024]{1,0:T(8,128)S(1)} %get-tuple-element.877, f32[128,1024]{1,0:T(8,128)S(1)} %get-tuple-element.878, f32[16,1024]{1,0:T(8,128)S(1)} %get-tuple-element.879, f32[128,1024]{1,0:T(8,128)S(1)} %get-tuple-element.880), kind=kLoop, calls=%fused_computation.5.clone.1 | loop fusion | flops 16777216 | bytes 9568256 | tf_op jit(solution)/shard_map/convert.3
  269.4 7.4 %bitcast_dynamic-update-slice_fusion.2 = (f32[6,2048,128]{1,2,0:T(8,128)}, f32[2048,128]{0,1:T(8,128)S(1)}) fusion(f32[6,2048,128]{1,2,0:T(8,128)} %get-tuple-element.934, s32[]{:T(128)S(6)} %select_n.258, f32[128]{0:T(128)S(1)} %multiply_bitcast_fusion.2, bf16[1,128,2048]{2,1,0:T(8,128)(2,1)S(1)} %get-tuple-element.958, ...), kind=kOutput, calls=%fused_computation.8.clone.1 | convolution fusion | flops 1091043328 | bytes 11010564 | tf_op jit(solution)/shard_map/while/body/dot_general | solution.py:53
  277.7 16.7 %all-gather = f32[2048,8]{0,1:T(8,128)S(1)} all-gather(f32[128,8]{0,1:T(8,128)S(1)} %get-tuple-element.540), channel_id=2, replica_groups=mesh['grp'=2,'orient'=16] {'orient'}, dimensions={0}, use_global_device_ids=true | all-gather | bytes 69632 | tf_op jit(solution)/shard_map/all_gather | solution.py:15
  294.4 19.8 %all-gather.1 = f32[2048,8]{0,1:T(8,128)S(1)} all-gather(f32[128,8]{0,1:T(8,128)S(1)} %get-tuple-element.541), channel_id=3, replica_groups=mesh['grp'=2,'orient'=16] {'orient'}, dimensions={0}, use_global_device_ids=true | all-gather | bytes 69632 | tf_op jit(solution)/shard_map/all_gather | solution.py:15
  315.1 122.0 %while.51 = (s32[]{:T(128)}, f32[1,128,2048]{2,1,0:T(8,128)S(1)}, f32[1,128]{1,0:T(1,128)S(1)}, s32[]{:T(128)}, f32[6,2048,128]{1,2,0:T(8,128)}, /*index=5*/s32[...) while((s32[]{:T(128)}, f32[1,128,2048]{2,1,0:T(8,128)S(1)}, ...), condition=%wide.region_11.12_spmd, body=%wide.region_9.11_spmd.sunk | while | flops 1109998848 | bytes 29153852 | solution.py:157
  323.8 4.8 %subtract_convert_fusion.5 = (bf16[16,128,1024]{2,1,0:T(8,128)(2,1)}, bf16[16,128,1024]{2,1,0:T(8,128)(2,1)}) fusion(f32[16,1024]{1,0:T(8,128)S(1)} %get-tuple-element.909, f32[128,1024]{1,0:T(8,128)S(1)} %get-tuple-element.910, f32[16,1024]{1,0:T(8,128)S(1)} %get-tuple-element.911, f32[128,1024]{1,0:T(8,128)S(1)} %get-tuple-element.912), kind=kLoop, calls=%fused_computation.57.clone.1 | loop fusion | flops 16777216 | bytes 9568256 | tf_op jit(solution)/shard_map/convert.4
  330.2 4.5 %fusion.84 = f32[1,128,2048]{2,1,0:T(8,128)S(1)} fusion(bf16[16,128,1024]{2,1,0:T(8,128)(2,1)} %get-tuple-element.913, bf16[16,128,1024]{2,1,0:T(8,128)(2,1)} %get-tuple-element.914, f32[1,128,2048]{2,1,0:T(8,128)S(1)} %get-tuple-element.1005, f32[16,128,128]{2,1,0:T(8,128)S(1)} %bitcast.141, f32[128]{0:T(128)S(1)} %get-tuple-element.915, ...), kind=kOutput, calls=%fused_computation.60.clone.1 | convolution fusion | flops 1091567616 | bytes 11535360 | tf_op jit(solution)/shard_map/while/body/dot_general | solution.py:140
  344.0 4.8 %subtract_convert_fusion.5 = (bf16[16,128,1024]{2,1,0:T(8,128)(2,1)}, bf16[16,128,1024]{2,1,0:T(8,128)(2,1)}) fusion(f32[16,1024]{1,0:T(8,128)S(1)} %get-tuple-element.909, f32[128,1024]{1,0:T(8,128)S(1)} %get-tuple-element.910, f32[16,1024]{1,0:T(8,128)S(1)} %get-tuple-element.911, f32[128,1024]{1,0:T(8,128)S(1)} %get-tuple-element.912), kind=kLoop, calls=%fused_computation.57.clone.1 | loop fusion | flops 16777216 | bytes 9568256 | tf_op jit(solution)/shard_map/convert.4
  350.4 4.5 %fusion.84 = f32[1,128,2048]{2,1,0:T(8,128)S(1)} fusion(bf16[16,128,1024]{2,1,0:T(8,128)(2,1)} %get-tuple-element.913, bf16[16,128,1024]{2,1,0:T(8,128)(2,1)} %get-tuple-element.914, f32[1,128,2048]{2,1,0:T(8,128)S(1)} %get-tuple-element.1005, f32[16,128,128]{2,1,0:T(8,128)S(1)} %bitcast.141, f32[128]{0:T(128)S(1)} %get-tuple-element.915, ...), kind=kOutput, calls=%fused_computation.60.clone.1 | convolution fusion | flops 1091567616 | bytes 11535360 | tf_op jit(solution)/shard_map/while/body/dot_general | solution.py:140
  364.2 4.8 %subtract_convert_fusion.5 = (bf16[16,128,1024]{2,1,0:T(8,128)(2,1)}, bf16[16,128,1024]{2,1,0:T(8,128)(2,1)}) fusion(f32[16,1024]{1,0:T(8,128)S(1)} %get-tuple-element.909, f32[128,1024]{1,0:T(8,128)S(1)} %get-tuple-element.910, f32[16,1024]{1,0:T(8,128)S(1)} %get-tuple-element.911, f32[128,1024]{1,0:T(8,128)S(1)} %get-tuple-element.912), kind=kLoop, calls=%fused_computation.57.clone.1 | loop fusion | flops 16777216 | bytes 9568256 | tf_op jit(solution)/shard_map/convert.4
  370.6 4.5 %fusion.84 = f32[1,128,2048]{2,1,0:T(8,128)S(1)} fusion(bf16[16,128,1024]{2,1,0:T(8,128)(2,1)} %get-tuple-element.913, bf16[16,128,1024]{2,1,0:T(8,128)(2,1)} %get-tuple-element.914, f32[1,128,2048]{2,1,0:T(8,128)S(1)} %get-tuple-element.1005, f32[16,128,128]{2,1,0:T(8,128)S(1)} %bitcast.141, f32[128]{0:T(128)S(1)} %get-tuple-element.915, ...), kind=kOutput, calls=%fused_computation.60.clone.1 | convolution fusion | flops 1091567616 | bytes 11535360 | tf_op jit(solution)/shard_map/while/body/dot_general | solution.py:140
  384.4 4.8 %subtract_convert_fusion.5 = (bf16[16,128,1024]{2,1,0:T(8,128)(2,1)}, bf16[16,128,1024]{2,1,0:T(8,128)(2,1)}) fusion(f32[16,1024]{1,0:T(8,128)S(1)} %get-tuple-element.909, f32[128,1024]{1,0:T(8,128)S(1)} %get-tuple-element.910, f32[16,1024]{1,0:T(8,128)S(1)} %get-tuple-element.911, f32[128,1024]{1,0:T(8,128)S(1)} %get-tuple-element.912), kind=kLoop, calls=%fused_computation.57.clone.1 | loop fusion | flops 16777216 | bytes 9568256 | tf_op jit(solution)/shard_map/convert.4
  390.8 4.5 %fusion.84 = f32[1,128,2048]{2,1,0:T(8,128)S(1)} fusion(bf16[16,128,1024]{2,1,0:T(8,128)(2,1)} %get-tuple-element.913, bf16[16,128,1024]{2,1,0:T(8,128)(2,1)} %get-tuple-element.914, f32[1,128,2048]{2,1,0:T(8,128)S(1)} %get-tuple-element.1005, f32[16,128,128]{2,1,0:T(8,128)S(1)} %bitcast.141, f32[128]{0:T(128)S(1)} %get-tuple-element.915, ...), kind=kOutput, calls=%fused_computation.60.clone.1 | convolution fusion | flops 1091567616 | bytes 11535360 | tf_op jit(solution)/shard_map/while/body/dot_general | solution.py:140
  404.6 4.8 %subtract_convert_fusion.5 = (bf16[16,128,1024]{2,1,0:T(8,128)(2,1)}, bf16[16,128,1024]{2,1,0:T(8,128)(2,1)}) fusion(f32[16,1024]{1,0:T(8,128)S(1)} %get-tuple-element.909, f32[128,1024]{1,0:T(8,128)S(1)} %get-tuple-element.910, f32[16,1024]{1,0:T(8,128)S(1)} %get-tuple-element.911, f32[128,1024]{1,0:T(8,128)S(1)} %get-tuple-element.912), kind=kLoop, calls=%fused_computation.57.clone.1 | loop fusion | flops 16777216 | bytes 9568256 | tf_op jit(solution)/shard_map/convert.4
  411.0 4.5 %fusion.84 = f32[1,128,2048]{2,1,0:T(8,128)S(1)} fusion(bf16[16,128,1024]{2,1,0:T(8,128)(2,1)} %get-tuple-element.913, bf16[16,128,1024]{2,1,0:T(8,128)(2,1)} %get-tuple-element.914, f32[1,128,2048]{2,1,0:T(8,128)S(1)} %get-tuple-element.1005, f32[16,128,128]{2,1,0:T(8,128)S(1)} %bitcast.141, f32[128]{0:T(128)S(1)} %get-tuple-element.915, ...), kind=kOutput, calls=%fused_computation.60.clone.1 | convolution fusion | flops 1091567616 | bytes 11535360 | tf_op jit(solution)/shard_map/while/body/dot_general | solution.py:140
  424.8 4.8 %subtract_convert_fusion.5 = (bf16[16,128,1024]{2,1,0:T(8,128)(2,1)}, bf16[16,128,1024]{2,1,0:T(8,128)(2,1)}) fusion(f32[16,1024]{1,0:T(8,128)S(1)} %get-tuple-element.909, f32[128,1024]{1,0:T(8,128)S(1)} %get-tuple-element.910, f32[16,1024]{1,0:T(8,128)S(1)} %get-tuple-element.911, f32[128,1024]{1,0:T(8,128)S(1)} %get-tuple-element.912), kind=kLoop, calls=%fused_computation.57.clone.1 | loop fusion | flops 16777216 | bytes 9568256 | tf_op jit(solution)/shard_map/convert.4
  431.2 4.5 %fusion.84 = f32[1,128,2048]{2,1,0:T(8,128)S(1)} fusion(bf16[16,128,1024]{2,1,0:T(8,128)(2,1)} %get-tuple-element.913, bf16[16,128,1024]{2,1,0:T(8,128)(2,1)} %get-tuple-element.914, f32[1,128,2048]{2,1,0:T(8,128)S(1)} %get-tuple-element.1005, f32[16,128,128]{2,1,0:T(8,128)S(1)} %bitcast.141, f32[128]{0:T(128)S(1)} %get-tuple-element.915, ...), kind=kOutput, calls=%fused_computation.60.clone.1 | convolution fusion | flops 1091567616 | bytes 11535360 | tf_op jit(solution)/shard_map/while/body/dot_general | solution.py:140
  (250 shorter events, 96.5 us)
Async XLA Ops:
  0.6 141.8 %copy-start.2 = (bf16[64,2048]{1,0:T(8,128)(2,1)S(1)}, bf16[64,2048]{1,0:T(8,128)(2,1)}, u32[]{:S(2)}) copy-start(bf16[64,2048]{1,0:T(8,128)(2,1)} %param.11) | copy-start | bytes 786436
  0.6 4.3 collective-permute-start
  4.9 42.2 %copy-start.3 = (bf16[64,2048]{1,0:T(8,128)(2,1)}, bf16[64,2048]{1,0:T(8,128)(2,1)S(1)}, u32[]{:S(2)}) copy-start(bf16[64,2048]{1,0:T(8,128)(2,1)S(1)} %collective-permute-done) | copy-start | bytes 786436
  6.0 14.2 %collective-permute-start.1 = (bf16[128,2048]{1,0:T(8,128)(2,1)S(1)}, bf16[128,2048]{1,0:T(8,128)(2,1)S(1)}, u32[]{:S(2)}, u32[]{:S(2)}) collective-permute-start(bf16[128,2048]{1,0:T(8,128)(2,1)S(1)} %pad_maximum_fusion.2), channel_id=1, source_target_pairs={{0,14},{1,15},{2,0},{3,1},{4,2},{5,3},{6,4},{7,5},{8,6},{9,7},{10,... | collective-permute-start | bytes 1572872 | tf_op jit(solution)/shard_map/ppermute | solution.py:82
  20.2 26.9 %copy-start = (bf16[128,2048]{1,0:T(8,128)(2,1)}, bf16[128,2048]{1,0:T(8,128)(2,1)S(1)}, u32[]{:S(2)}) copy-start(bf16[128,2048]{1,0:T(8,128)(2,1)S(1)} %collective-permute-done.1) | copy-start | bytes 1572868
  21.4 25.7 %collective-permute-start.2 = (bf16[256,2048]{1,0:T(8,128)(2,1)S(1)}, bf16[256,2048]{1,0:T(8,128)(2,1)S(1)}, u32[]{:S(2)}, u32[]{:S(2)}) collective-permute-start(bf16[256,2048]{1,0:T(8,128)(2,1)S(1)} %pad_maximum_fusion.1), channel_id=1, source_target_pairs={{0,12},{1,13},{2,14},{3,15},{4,0},{5,1},{6,2},{7,3},{8,4},{9,5},{1... | collective-permute-start | bytes 3145736 | tf_op jit(solution)/shard_map/ppermute | solution.py:82
  49.5 92.7 %collective-permute-start.3 = (bf16[512,2048]{1,0:T(8,128)(2,1)}, bf16[512,2048]{1,0:T(8,128)(2,1)S(1)}, u32[]{:S(2)}, u32[]{:S(2)}) collective-permute-start(bf16[512,2048]{1,0:T(8,128)(2,1)} %pad_maximum_fusion), channel_id=1, source_target_pairs={{0,8},{1,9},{2,10},{3,11},{4,12},{5,13},{6,14},{7,15},{8,0},{9,1},... | collective-permute-start | bytes 6291464 | tf_op jit(solution)/shard_map/ppermute | solution.py:82
  49.9 92.6 %copy-start.4 = (bf16[64,2048]{1,0:T(8,128)(2,1)S(1)}, bf16[64,2048]{1,0:T(8,128)(2,1)}, u32[]{:S(2)}) copy-start(bf16[64,2048]{1,0:T(8,128)(2,1)} %copy-done.3) | copy-start | bytes 786436
  49.9 92.6 %copy-start.1 = (bf16[128,2048]{1,0:T(8,128)(2,1)S(1)}, bf16[128,2048]{1,0:T(8,128)(2,1)}, u32[]{:S(2)}) copy-start(bf16[128,2048]{1,0:T(8,128)(2,1)} %copy-done) | copy-start | bytes 1572868
  143.3 7.8 %copy-start.6 = (bf16[128,2048]{1,0:T(8,128)(2,1)S(1)}, bf16[128,2048]{1,0:T(8,128)(2,1)}, u32[]{:S(2)}) copy-start(bf16[128,2048]{1,0:T(8,128)(2,1)} %param.12) | copy-start | bytes 1572868
  437.2 1.0 copy-start.5
  437.2 1.0 copy-start.7
